TPU v7x, 512 devices: a whole 4x8x8 slice. The times are simulated.
512 devices in a mesh: gx: 64 (over x, z_lo, y), gy: 8 (over z_hi, core).
Axes of the slice: x: 4, y: 8, z: 8 (z_hi: 4, z_lo: 2; z = z_hi * 2 + z_lo), core: 2. Of those that a mesh axis runs over, the one named last changes fastest.
Arguments:
- flow_field: bfloat16 [256, 128, 64, 128], P('gx', 'gy'), may hold values from -6 to 6
- spectral_weight: bfloat16 [512, 64, 2, 64, 128], P(('gy', 'gx')), may hold values from -1 to 1
- conv_weight: bfloat16 [3, 3, 3, 128, 128], replicated, may hold values from -0.109375 to 0.109375
- channel_bias: float32 [128], replicated, may hold values from -3 to 3
Outputs:
- activated: bfloat16 [256, 128, 64, 128], P('gx', 'gy')
All inputs are finite; a program needn't handle non-finite values.
Results may differ from a plain program's by a relative error of at most 0.018.
Values may be sent and summed in bfloat16 or wider, within the bound.
A program may use at most 128 MiB of HBM per device.

v0:
```python
import math
import jax
import jax.numpy as jnp
from jax import lax
from jax.sharding import PartitionSpec as P

MX = 64
MY = 16
MZ = 16


def with_halo(array, sides, width):
    for axis, dim in sides:
        size, length = (lax.axis_size(axis), array.shape[dim])
        up = [(i, (i + 1) % size) for i in range(size - 1)]
        down = [(j, i) for i, j in up]
        last = lax.slice_in_dim(array, length - width, length, axis=dim)
        initial = lax.slice_in_dim(array, 0, width, axis=dim)
        before = lax.ppermute(last, axis, up)
        after = lax.ppermute(initial, axis, down)
        array = jnp.concatenate([before, array, after], axis=dim)
    return array


def signed_modes(mode_count):
    position = jnp.arange(mode_count, dtype=jnp.int32)
    return jnp.where(position < mode_count // 2, position, position - mode_count)


def angle_grid(first, second, length):
    phase_turns = first[:, None] * second[None, :] % length
    return phase_turns.astype(jnp.float32) * (2.0 * math.pi / length)


def real_table(first, second, length, factor):
    angles = angle_grid(first, second, length)
    return jnp.stack([jnp.cos(angles) * factor, -jnp.sin(angles) * factor])


def complex_table(first, second, length, factor, direction):
    angles = angle_grid(first, second, length)
    cosine = jnp.cos(angles) * factor
    sine_part = jnp.sin(angles) * factor
    return jnp.stack(
        [jnp.stack([cosine, direction * sine_part]), jnp.stack([-direction * sine_part, cosine])]
    )


def spectral_part(flow_field, spectral_weight):
    highest = lax.Precision.HIGHEST
    cells_x, cells_y, cells_z, channels = flow_field.shape
    count_x = lax.axis_size("gx")
    count_y = lax.axis_size("gy")
    full_x = cells_x * count_x
    full_y = cells_y * count_y
    item_count = spectral_weight.shape[0]
    local_y = lax.axis_index("gy") * cells_y + jnp.arange(cells_y, dtype=jnp.int32)
    grid_x = jnp.arange(full_x, dtype=jnp.int32)
    grid_z = jnp.arange(cells_z, dtype=jnp.int32)
    modes_z = jnp.arange(MZ, dtype=jnp.int32)
    forward_z = real_table(grid_z, modes_z, cells_z, cells_z ** (-0.5)).astype(jnp.bfloat16)
    z_spectrum = jnp.einsum(
        "xyzc,pzk->pxykc", flow_field, forward_z, preferred_element_type=jnp.float32
    )
    forward_y = complex_table(local_y, signed_modes(MY), full_y, full_y ** (-0.5), -1.0)
    y_partial = jnp.einsum("pxykc,pqyj->qxjkc", z_spectrum, forward_y, precision=highest)
    y_partial = y_partial.reshape(2, cells_x, count_y, count_x, item_count, channels // 2)
    owned = lax.psum_scatter(
        y_partial.astype(jnp.bfloat16), "gy", scatter_dimension=2, tiled=True
    ).astype(jnp.float32)
    owned_modes = owned.reshape(2, cells_x, count_x, item_count, channels // 2)
    gathered_rows = lax.all_to_all(
        owned_modes.astype(jnp.bfloat16), "gx", split_axis=2, concat_axis=1, tiled=True
    ).astype(owned_modes.dtype)
    gathered_rows = gathered_rows.reshape(2, full_x, item_count, channels // 2)
    forward_x = complex_table(grid_x, signed_modes(MX), full_x, full_x ** (-0.5), -1.0)
    x_spectrum = jnp.einsum("pxjc,pqxm->qmjc", gathered_rows, forward_x, precision=highest).astype(
        jnp.bfloat16
    )
    products = jnp.einsum(
        "pmjc,jmqco->pqmjo", x_spectrum, spectral_weight, preferred_element_type=jnp.float32
    )
    mixed_modes = jnp.stack([products[0, 0] - products[1, 1], products[0, 1] + products[1, 0]])
    backward_x = complex_table(signed_modes(MX), grid_x, full_x, MX ** (-0.5), 1.0)
    inverse_x = jnp.einsum("pmjc,pqmx->qxjc", mixed_modes, backward_x, precision=highest)
    inverse_x = inverse_x.reshape(2, full_x, 1, item_count, channels)
    returned = lax.all_to_all(
        inverse_x.astype(jnp.bfloat16), "gx", split_axis=1, concat_axis=2, tiled=True
    ).astype(inverse_x.dtype)
    band_rows = MY // count_y
    summed = returned.reshape(2, cells_x, band_rows * MZ, 2, channels).sum(axis=3)
    summed = summed.reshape(2, cells_x, band_rows, MZ, channels)
    coefficients = lax.all_gather(summed.astype(jnp.bfloat16), "gy", axis=2, tiled=True).astype(
        summed.dtype
    )
    backward_y = complex_table(signed_modes(MY), local_y, full_y, MY ** (-0.5), 1.0)
    y_inverse = jnp.einsum("pxjkc,pqjy->qxykc", coefficients, backward_y, precision=highest).astype(
        jnp.bfloat16
    )
    backward_z = real_table(modes_z, grid_z, cells_z, MZ ** (-0.5)).astype(jnp.bfloat16)
    return jnp.einsum("pxykc,pkz->xyzc", y_inverse, backward_z, preferred_element_type=jnp.float32)


def convolve(flow_field, conv_weight):
    cells_x, cells_y, cells_z, channels = flow_field.shape
    padded = with_halo(flow_field, (("gx", 0), ("gy", 1)), 1)
    padded = jnp.pad(padded, ((0, 0), (0, 0), (1, 1), (0, 0)))
    stacked = jnp.concatenate(
        [padded[:, :, 0:cells_z], padded[:, :, 1 : cells_z + 1], padded[:, :, 2 : cells_z + 2]],
        axis=3,
    )
    kernel = conv_weight.reshape(3, 3, 3 * channels, channels)
    accumulated = jnp.zeros((cells_x, cells_y, cells_z, channels), jnp.float32)
    for shift_x in range(3):
        for shift_y in range(3):
            accumulated = accumulated + jnp.dot(
                stacked[shift_x : shift_x + cells_x, shift_y : shift_y + cells_y],
                kernel[shift_x, shift_y],
                preferred_element_type=jnp.float32,
            )
    return accumulated


def body(flow_field, spectral_weight, conv_weight, channel_bias):
    convolved = convolve(flow_field, conv_weight)
    spectral = spectral_part(flow_field, spectral_weight)
    return jax.nn.gelu(spectral + convolved + channel_bias, approximate=True).astype(jnp.bfloat16)


def solution(mesh):
    placed = (P("gx", "gy", None, None), P(("gy", "gx"), None, None, None, None), P(), P())
    return jax.shard_map(
        body, mesh=mesh, in_specs=placed, out_specs=P("gx", "gy", None, None), check_vma=False
    )
```

profile of v0, /device:TPU:1, one launch (start us, length us, event | category | flops | bytes accessed | tf_op | source)
XLA Modules:
  0.0 191.2 jit_solution(16741173766615642969)
XLA Ops:
  6.5 2.0 %fusion.100 = (bf16[1,16,64,128]{3,2,1,0:T(8,128)(2,1)}, bf16[1,16,64,128]{3,2,1,0:T(8,128)(2,1)}) fusion(bf16[4,16,64,128]{3,2,1,0:T(8,128)(2,1)} %param.4), kind=kLoop, calls=%fused_computation.177 | loop fusion | bytes 1048576 | tf_op jit(solution)/shard_map/slice | solution.py:18
  8.6 1.3 collective-permute-start.1
  9.9 5.4 %collective-permute-start = (bf16[1,16,64,128]{3,2,1,0:T(8,128)(2,1)}, bf16[1,16,64,128]{3,2,1,0:T(8,128)(2,1)}, u32[]{:S(2)}, u32[]{:S(2)}) collective-permute-start(bf16[1,16,64,128]{3,2,1,0:T(8,128)(2,1)} %get-tuple-element.10), channel_id=1, source_target_pairs={{0,8},{8,16},{16,24},{24,32},{32,40},{40,48},{48,56},{56,64},{64,7... | collective-permute-start | bytes 786440 | tf_op jit(solution)/shard_map/ppermute | solution.py:19
  15.3 0.8 broadcast_multiply_fusion.7
  16.1 1.5 convolution_bitcast_fusion.2
  17.6 1.2 fusion.20
  18.8 1.0 copy.48
  19.8 2.5 %convert_element_type.204 = bf16[2,4,8,64,1,64]{5,3,2,1,0,4:T(8,128)(2,1)} reshape(bf16[2,4,16,16,128]{4,3,2,1,0:T(8,128)(2,1)} %copy.48) | data formatting | bytes 1048576 | tf_op jit(solution)/shard_map/convert_element_type | solution.py:69
  22.3 0.3 broadcast_multiply_fusion.3
  22.6 0.3 broadcast_multiply_fusion
  23.0 0.7 maximum_bitcast_fusion.2
  23.7 1.4 maximum_bitcast_fusion.9
  25.1 1.3 dynamic-slice
  26.3 1.0 constant_dynamic-update-slice_fusion.2
  27.5 1.0 constant_dynamic-update-slice_fusion
  28.5 7.1 %collective-permute-start.2 = (bf16[6,1,64,128]{3,2,1,0:T(8,128)(2,1)S(1)}, bf16[6,1,64,128]{3,2,1,0:T(8,128)(2,1)S(1)}, u32[]{:S(2)}, u32[]{:S(2)}) collective-permute-start(bf16[6,1,64,128]{3,2,1,0:T(8,128)(2,1)S(1)} %get-tuple-element.7), channel_id=1, source_target_pairs={{0,1},{1,2},{2,3},{3,4},{4,5},{5,6},{6,7},{8,9},{9,10},{10,11},{11... | collective-permute-start | bytes 294920 | tf_op jit(solution)/shard_map/ppermute | solution.py:19
  35.6 2.9 %collective-permute-start.3 = (bf16[6,1,64,128]{3,2,1,0:T(8,128)(2,1)S(1)}, bf16[6,1,64,128]{3,2,1,0:T(8,128)(2,1)S(1)}, u32[]{:S(2)}, u32[]{:S(2)}) collective-permute-start(bf16[6,1,64,128]{3,2,1,0:T(8,128)(2,1)S(1)} %get-tuple-element.8), channel_id=1, source_target_pairs={{1,0},{2,1},{3,2},{4,3},{5,4},{6,5},{7,6},{9,8},{10,9},{11,10},{12... | collective-permute-start | bytes 294920 | tf_op jit(solution)/shard_map/ppermute | solution.py:20
  38.5 0.7 multiply_convert_fusion.2
  39.1 3.3 %collective-permute-done.3 = bf16[6,1,64,128]{3,2,1,0:T(8,128)(2,1)S(1)} collective-permute-done((bf16[6,1,64,128]{3,2,1,0:T(8,128)(2,1)S(1)}, bf16[6,1,64,128]{3,2,1,0:T(8,128)(2,1)S(1)}, u32[]{:S(2)}, u32[]{:S(2)}) %collective-permute-start.3) | collective-permute-done | bytes 98336 | tf_op jit(solution)/shard_map/ppermute | solution.py:20
  42.4 1.2 fusion.16
  43.7 0.9 fusion.98
  44.6 0.9 pad_maximum_fusion
  45.5 0.3 copy-done.5
  45.8 2.7 %fusion.41 = f32[4,16,64,128]{3,2,1,0:T(8,128)} fusion(bf16[6,18,64,384]{3,2,1,0:T(8,128)(2,1)S(1)} %pad_maximum_fusion, bf16[3,3,384,128]{3,2,1,0:T(8,128)(2,1)S(1)} %bitcast.222), kind=kOutput, calls=%fused_computation.56 | convolution fusion | flops 402653184 | bytes 7503872 | tf_op jit(solution)/shard_map/dot_general | solution.py:116
  48.5 2.3 %fusion.42 = f32[4,16,64,128]{3,2,1,0:T(8,128)} fusion(bf16[6,18,64,384]{3,2,1,0:T(8,128)(2,1)S(1)} %pad_maximum_fusion, bf16[3,3,384,128]{3,2,1,0:T(8,128)(2,1)S(1)} %bitcast.223), kind=kOutput, calls=%fused_computation.58 | convolution fusion | flops 402653184 | bytes 7503872 | tf_op jit(solution)/shard_map/dot_general | solution.py:116
  50.8 2.3 %fusion.43 = f32[4,16,64,128]{3,2,1,0:T(8,128)} fusion(bf16[6,18,64,384]{3,2,1,0:T(8,128)(2,1)S(1)} %pad_maximum_fusion, bf16[3,3,384,128]{3,2,1,0:T(8,128)(2,1)S(1)} %bitcast.224), kind=kOutput, calls=%fused_computation.60 | convolution fusion | flops 402653184 | bytes 7503872 | tf_op jit(solution)/shard_map/dot_general | solution.py:116
  53.1 2.4 %fusion.44 = f32[4,16,64,128]{3,2,1,0:T(8,128)} fusion(bf16[6,18,64,384]{3,2,1,0:T(8,128)(2,1)S(1)} %pad_maximum_fusion, bf16[3,3,384,128]{3,2,1,0:T(8,128)(2,1)S(1)} %bitcast.225), kind=kOutput, calls=%fused_computation.62 | convolution fusion | flops 402653184 | bytes 7503872 | tf_op jit(solution)/shard_map/dot_general | solution.py:116
  55.5 2.3 %fusion.45 = f32[4,16,64,128]{3,2,1,0:T(8,128)} fusion(bf16[6,18,64,384]{3,2,1,0:T(8,128)(2,1)S(1)} %pad_maximum_fusion, bf16[3,3,384,128]{3,2,1,0:T(8,128)(2,1)S(1)} %bitcast.226), kind=kOutput, calls=%fused_computation.64 | convolution fusion | flops 402653184 | bytes 7503872 | tf_op jit(solution)/shard_map/dot_general | solution.py:116
  57.8 2.4 %fusion.46 = f32[4,16,64,128]{3,2,1,0:T(8,128)} fusion(bf16[6,18,64,384]{3,2,1,0:T(8,128)(2,1)S(1)} %pad_maximum_fusion, bf16[3,3,384,128]{3,2,1,0:T(8,128)(2,1)S(1)} %bitcast.227), kind=kOutput, calls=%fused_computation.66 | convolution fusion | flops 402653184 | bytes 7503872 | tf_op jit(solution)/shard_map/dot_general | solution.py:116
  60.2 49.9 %all-reduce.4.cloned.1.call-done = bf16[2,4,8,64,1,64]{5,3,2,1,0,4:T(8,128)(2,1)} async-done(((bf16[2,4,8,64,1,64]{5,3,2,1,0,4:T(8,128)(2,1)}), bf16[2,4,8,64,1,64]{5,3,2,1,0,4:T(8,128)(2,1)}) %all-reduce.4.cloned.1.call-update) | async-done | bytes 524304
  110.1 1.5 dynamic-slice_bitcast_fusion
  111.6 0.8 copy.109
  112.4 1.7 reshape.950
  114.1 10.7 %all-to-all-start = ((bf16[64,2,256]{2,1,0:T(2,128)(2,1)}), bf16[64,2,256]{2,1,0:T(2,128)(2,1)}, u32[]{:S(2)}, u32[]{:S(2)}) async-start(bf16[64,2,256]{2,1,0:T(2,128)(2,1)} %reshape.950), calls=%async_computation | async-start | bytes 131072 | tf_op jit(solution)/shard_map/all_to_all | solution.py:72
  124.8 4.2 %fusion.47 = f32[4,16,64,128]{3,2,1,0:T(8,128)} fusion(bf16[6,18,64,384]{3,2,1,0:T(8,128)(2,1)} %copy-done.1, bf16[3,3,384,128]{3,2,1,0:T(8,128)(2,1)S(1)} %bitcast.228), kind=kOutput, calls=%fused_computation.68 | convolution fusion | flops 402653184 | bytes 7503872 | tf_op jit(solution)/shard_map/dot_general | solution.py:116
  129.0 4.9 %all-to-all-done = bf16[64,2,256]{2,1,0:T(2,128)(2,1)} async-done(((bf16[64,2,256]{2,1,0:T(2,128)(2,1)}), bf16[64,2,256]{2,1,0:T(2,128)(2,1)}, u32[]{:S(2)}, u32[]{:S(2)}) %all-to-all-start) | async-done | bytes 65568 | tf_op jit(solution)/shard_map/all_to_all | solution.py:72
  134.0 1.7 reshape.951
  135.6 0.9 bitcast_bitcast_fusion
  136.9 0.4 fusion.23
  137.4 0.6 fusion.22
  138.0 0.8 copy.55
  138.8 5.7 %all-to-all-start.1 = ((bf16[2,256,1,1,128]{4,0,3,2,1:T(2,128)(2,1)}), bf16[2,256,1,1,128]{4,0,3,2,1:T(2,128)(2,1)S(1)}, u32[]{:S(2)}, u32[]{:S(2)}) async-start(bf16[2,256,1,1,128]{4,0,3,2,1:T(2,128)(2,1)} %copy.55), calls=%async_computation.1 | async-start | bytes 262144 | tf_op jit(solution)/shard_map/all_to_all | solution.py:87
  144.5 4.2 %fusion.48 = f32[4,16,64,128]{3,2,1,0:T(8,128)} fusion(bf16[6,18,64,384]{3,2,1,0:T(8,128)(2,1)} %copy-done.1, bf16[3,3,384,128]{3,2,1,0:T(8,128)(2,1)S(1)} %bitcast.229), kind=kOutput, calls=%fused_computation.70 | convolution fusion | flops 402653184 | bytes 7503872 | tf_op jit(solution)/shard_map/dot_general | solution.py:116
  148.7 5.8 %all-to-all-done.1 = bf16[2,256,1,1,128]{4,0,3,2,1:T(2,128)(2,1)S(1)} async-done(((bf16[2,256,1,1,128]{4,0,3,2,1:T(2,128)(2,1)}), bf16[2,256,1,1,128]{4,0,3,2,1:T(2,128)(2,1)S(1)}, u32[]{:S(2)}, u32[]{:S(2)}) %all-to-all-start.1) | async-done | bytes 131104 | tf_op jit(solution)/shard_map/all_to_all | solution.py:87
  154.7 19.6 %all_gather.3 = bf16[2,4,16,16,128]{4,3,1,0,2:T(8,128)(2,1)S(1)} all-gather(bf16[2,4,2,16,128]{4,3,1,0,2:T(8,128)(2,1)S(1)} %copy.58), channel_id=1, replica_groups=mesh['gx'=64,'gy'=8] {'gy'}, dimensions={2}, use_global_device_ids=true | all-gather | bytes 589824 | tf_op jit(solution)/shard_map/all_gather | solution.py:93
  174.3 0.7 fusion.19
  175.1 0.5 fusion.32
  175.6 8.8 %fusion.11 = bf16[4,16,64,128]{3,2,1,0:T(8,128)(2,1)} fusion(f32[64,4,16,128,1]{3,0,4,2,1:T(8,128)S(1)} %fusion.32, f32[4,16,64,128]{3,2,1,0:T(8,128)S(1)} %copy-done.2, f32[4,16,64,128]{3,2,1,0:T(8,128)S(1)} %copy-done.3, f32[4,16,64,128]{3,2,1,0:T(8,128)} %fusion.43, f32[4,16,64,128]{3,2,1,0:T(8,128)} %fusion.44, f32[4,16,64,128]{3,2,1,0:T(8,128)} %fusion.45, ...), kind=kOutput, calls=%fused_computation.15 | convolution fusion | flops 412614656 | bytes 25330176 | tf_op jit(solution)/shard_map/dot_general | solution.py:116
  (40 shorter events, 0.9 us)
Async XLA Ops:
  6.5 130.4 %copy-start = (bf16[1,64,2,64,128]{4,3,2,1,0:T(8,128)(2,1)S(1)}, bf16[1,64,2,64,128]{4,3,2,1,0:T(8,128)(2,1)}, u32[]{:S(2)}) copy-start(bf16[1,64,2,64,128]{4,3,2,1,0:T(8,128)(2,1)} %param.5) | copy-start | bytes 6291460
  6.5 103.6 %all-reduce.4.cloned.1.call-start = ((), (), s32[]{:S(2)}) async-start(), calls=%async_computation.2 | async-start | bytes 2097152
  8.6 18.9 %collective-permute-start.1 = (bf16[1,16,64,128]{3,2,1,0:T(8,128)(2,1)}, bf16[1,16,64,128]{3,2,1,0:T(8,128)(2,1)}, u32[]{:S(2)}, u32[]{:S(2)}) collective-permute-start(bf16[1,16,64,128]{3,2,1,0:T(8,128)(2,1)} %get-tuple-element.9), channel_id=1, source_target_pairs={{8,0},{16,8},{24,16},{32,24},{40,32},{48,40},{56,48},{64,56},{72,6... | collective-permute-start | bytes 786440 | tf_op jit(solution)/shard_map/ppermute | solution.py:20
  9.9 16.5 %collective-permute-start = (bf16[1,16,64,128]{3,2,1,0:T(8,128)(2,1)}, bf16[1,16,64,128]{3,2,1,0:T(8,128)(2,1)}, u32[]{:S(2)}, u32[]{:S(2)}) collective-permute-start(bf16[1,16,64,128]{3,2,1,0:T(8,128)(2,1)} %get-tuple-element.10), channel_id=1, source_target_pairs={{0,8},{8,16},{16,24},{24,32},{32,40},{40,48},{48,56},{56,64},{64,7... | collective-permute-start | bytes 786440 | tf_op jit(solution)/shard_map/ppermute | solution.py:19
  19.8 7.5 %copy-start.4 = (bf16[4,16,64,128]{3,2,1,0:T(8,128)(2,1)S(1)}, bf16[4,16,64,128]{3,2,1,0:T(8,128)(2,1)}, u32[]{:S(2)}) copy-start(bf16[4,16,64,128]{3,2,1,0:T(8,128)(2,1)} %param.4) | copy-start | bytes 3145732
  28.5 10.6 %collective-permute-start.2 = (bf16[6,1,64,128]{3,2,1,0:T(8,128)(2,1)S(1)}, bf16[6,1,64,128]{3,2,1,0:T(8,128)(2,1)S(1)}, u32[]{:S(2)}, u32[]{:S(2)}) collective-permute-start(bf16[6,1,64,128]{3,2,1,0:T(8,128)(2,1)S(1)} %get-tuple-element.7), channel_id=1, source_target_pairs={{0,1},{1,2},{2,3},{3,4},{4,5},{5,6},{6,7},{8,9},{9,10},{10,11},{11... | collective-permute-start | bytes 294920 | tf_op jit(solution)/shard_map/ppermute | solution.py:19
  35.6 6.8 %collective-permute-start.3 = (bf16[6,1,64,128]{3,2,1,0:T(8,128)(2,1)S(1)}, bf16[6,1,64,128]{3,2,1,0:T(8,128)(2,1)S(1)}, u32[]{:S(2)}, u32[]{:S(2)}) collective-permute-start(bf16[6,1,64,128]{3,2,1,0:T(8,128)(2,1)S(1)} %get-tuple-element.8), channel_id=1, source_target_pairs={{1,0},{2,1},{3,2},{4,3},{5,4},{6,5},{7,6},{9,8},{10,9},{11,10},{12... | collective-permute-start | bytes 294920 | tf_op jit(solution)/shard_map/ppermute | solution.py:20
  44.6 1.2 copy-start.5
  45.5 12.4 %copy-start.1 = (bf16[6,18,64,384]{3,2,1,0:T(8,128)(2,1)}, bf16[6,18,64,384]{3,2,1,0:T(8,128)(2,1)S(1)}, u32[]{:S(2)}) copy-start(bf16[6,18,64,384]{3,2,1,0:T(8,128)(2,1)S(1)} %pad_maximum_fusion) | copy-start | bytes 15925252
  114.1 19.9 %all-to-all-start = ((bf16[64,2,256]{2,1,0:T(2,128)(2,1)}), bf16[64,2,256]{2,1,0:T(2,128)(2,1)}, u32[]{:S(2)}, u32[]{:S(2)}) async-start(bf16[64,2,256]{2,1,0:T(2,128)(2,1)} %reshape.950), calls=%async_computation | async-start | bytes 131072 | tf_op jit(solution)/shard_map/all_to_all | solution.py:72
  124.8 11.9 %copy-start.6 = (f32[1,2,256,64]{2,3,1,0:T(8,128)S(1)}, f32[1,2,256,64]{2,3,1,0:T(8,128)}, u32[]{:S(2)}) copy-start(f32[1,2,256,64]{2,3,1,0:T(8,128)} %get-tuple-element.15) | copy-start | bytes 393220
  138.8 15.7 %all-to-all-start.1 = ((bf16[2,256,1,1,128]{4,0,3,2,1:T(2,128)(2,1)}), bf16[2,256,1,1,128]{4,0,3,2,1:T(2,128)(2,1)S(1)}, u32[]{:S(2)}, u32[]{:S(2)}) async-start(bf16[2,256,1,1,128]{4,0,3,2,1:T(2,128)(2,1)} %copy.55), calls=%async_computation.1 | async-start | bytes 262144 | tf_op jit(solution)/shard_map/all_to_all | solution.py:87
  144.5 29.9 %copy-start.7 = (f32[1,2,16,16]{2,3,1,0:T(8,128)S(1)}, f32[1,2,16,16]{2,3,1,0:T(8,128)}, u32[]{:S(2)}) copy-start(f32[1,2,16,16]{2,3,1,0:T(8,128)} %get-tuple-element.19) | copy-start | bytes 6148
  148.7 26.4 %copy-start.8 = (bf16[1,16,64]{2,1,0:T(8,128)(2,1)S(1)}, bf16[1,16,64]{2,1,0:T(8,128)(2,1)}, u32[]{:S(2)}) copy-start(bf16[1,16,64]{2,1,0:T(8,128)(2,1)} %get-tuple-element.38) | copy-start | bytes 6148
  148.7 26.4 %copy-start.9 = (bf16[1,16,64]{2,1,0:T(8,128)(2,1)S(1)}, bf16[1,16,64]{2,1,0:T(8,128)(2,1)}, u32[]{:S(2)}) copy-start(bf16[1,16,64]{2,1,0:T(8,128)(2,1)} %get-tuple-element.39) | copy-start | bytes 6148
  154.7 20.8 %copy-start.2 = (f32[4,16,64,128]{3,2,1,0:T(8,128)S(1)}, f32[4,16,64,128]{3,2,1,0:T(8,128)}, u32[]{:S(2)}) copy-start(f32[4,16,64,128]{3,2,1,0:T(8,128)} %fusion.41) | copy-start | bytes 6291460
  154.7 20.8 %copy-start.3 = (f32[4,16,64,128]{3,2,1,0:T(8,128)S(1)}, f32[4,16,64,128]{3,2,1,0:T(8,128)}, u32[]{:S(2)}) copy-start(f32[4,16,64,128]{3,2,1,0:T(8,128)} %fusion.42) | copy-start | bytes 6291460
  154.7 20.8 %copy-start.10 = (f32[128]{0:T(128)S(1)}, f32[128]{0:T(128)}, u32[]{:S(2)}) copy-start(f32[128]{0:T(128)} %param.7) | copy-start | bytes 1540
Sparse Core Ops, SparseCore 0:
  22.4 87.7 all-reduce.3
where the time goes:
time: 192 us; the launch traced here: 191 us
  waiting for transfers between devices  64 us (33%)
  matrix products  36.8 us (19%)
  starting transfers between devices  33 us (17%)
  blocking collectives  19.6 us (10%)
  local copies, waits for them, and re-layouts  17.5 us (9%)
  between operations  13.8 us (7%)
  other arithmetic  6.65 us (3%)
    unnamed x2, waiting for transfers between devices  49.9 us
    dot_general x9, matrix products, convolve(): jnp.dot(stacked[shift_x:shift_x + cells_x, shift_y:shift_y + cells_y], ke...  31.7 us
    all_gather x1, blocking collectives, spectral_part(): lax.all_gather(summed.astype(jnp.bfloat16), 'gy', axis=2, tiled=True)  19.6 us
    ppermute x2, starting transfers between devices, with_halo(): before = lax.ppermute(last, axis, up)  12.5 us
    all_to_all x1, starting transfers between devices, spectral_part(): lax.all_to_all(owned_modes.astype(jnp.bfloat16), 'gx', split_axis=2, conc...  10.7 us
    unnamed x28, local copies, waits for them, and re-layouts  6.05 us
    all_to_all x1, waiting for transfers between devices, spectral_part(): lax.all_to_all(inverse_x.astype(jnp.bfloat16), 'gx', split_axis=1, concat...  5.77 us
    all_to_all x1, starting transfers between devices, spectral_part(): lax.all_to_all(inverse_x.astype(jnp.bfloat16), 'gx', split_axis=1, concat...  5.67 us
  transfers between devices with their start and end apart: 7, of which 4 were waited for; matrix products, arithmetic and copies ran while one was open for 21% of the time, Pallas kernels for 0%

commit v1 on v0

--- a/solution.py
+++ b/solution.py
@@ -90,9 +90,15 @@
     band_rows = MY // count_y
     summed = returned.reshape(2, cells_x, band_rows * MZ, 2, channels).sum(axis=3)
     summed = summed.reshape(2, cells_x, band_rows, MZ, channels)
-    coefficients = lax.all_gather(summed.astype(jnp.bfloat16), "gy", axis=2, tiled=True).astype(
-        summed.dtype
-    )
+    coefficients = jnp.concatenate(
+        lax.all_to_all(
+            jnp.stack(lax.psum(1, "gy") * [summed.astype(jnp.bfloat16)]),
+            split_axis=0,
+            axis_name="gy",
+            concat_axis=0,
+        ),
+        2,
+    ).astype(summed.dtype)
     backward_y = complex_table(signed_modes(MY), local_y, full_y, MY ** (-0.5), 1.0)
     y_inverse = jnp.einsum("pxjkc,pqjy->qxykc", coefficients, backward_y, precision=highest).astype(
         jnp.bfloat16

time: 192 us -> 199 us (1.036)
  blocking collectives: 19.6 us -> 0 us
  waiting for transfers between devices: 64 us -> 74.6 us
  starting transfers between devices: 33 us -> 41.2 us
  matrix products: 36.8 us -> 41.3 us
  local copies, waits for them, and re-layouts: 17.5 us -> 20.2 us
    all_gather x1 -> x0, blocking collectives: 19.6 us -> none  [spectral_part(): lax.all_gather(summed.astype(jnp.bfloat16), 'gy', axis=2, tiled=True)]
    all_to_all x0 -> x1, starting transfers between devices: none -> 8.22 us  [spectral_part(): lax.all_to_all(jnp.stack(lax.psum(1, 'gy') * [summed.astype(jnp.bfloat16)...]
    unnamed x2, waiting for transfers between devices: 49.9 us -> 57 us
    dot_general x9, matrix products: 31.7 us -> 36.3 us  [convolve(): jnp.dot(stacked[shift_x:shift_x + cells_x, shift_y:shift_y + cells_y], ke...]
    all_to_all x0 -> x1, waiting for transfers between devices: none -> 3.72 us  [spectral_part(): lax.all_to_all(jnp.stack(lax.psum(1, 'gy') * [summed.astype(jnp.bfloat16)...]
    unnamed x28 -> x32, local copies, waits for them, and re-layouts: 6.05 us -> 6.66 us
  transfers between devices with their start and end apart: 7 -> 8, of which waited for: 4 -> 5; matrix products, arithmetic and copies ran while one was open for 21% -> 22% of each run, Pallas kernels for 0% -> 0%
where the time goes in v1:
time: 199 us; the launch traced here: 198 us
  waiting for transfers between devices  74.6 us (37%)
  matrix products  41.3 us (21%)
  starting transfers between devices  41.2 us (21%)
  local copies, waits for them, and re-layouts  20.2 us (10%)
  between operations  13.7 us (7%)
  other arithmetic  6.63 us (3%)
    unnamed x2, waiting for transfers between devices  57 us
    dot_general x9, matrix products, convolve(): jnp.dot(stacked[shift_x:shift_x + cells_x, shift_y:shift_y + cells_y], ke...  36.3 us
    ppermute x2, starting transfers between devices, with_halo(): before = lax.ppermute(last, axis, up)  12.4 us
    all_to_all x1, starting transfers between devices, spectral_part(): lax.all_to_all(owned_modes.astype(jnp.bfloat16), 'gx', split_axis=2, conc...  10.7 us
    all_to_all x1, starting transfers between devices, spectral_part(): lax.all_to_all(jnp.stack(lax.psum(1, 'gy') * [summed.astype(jnp.bfloat16)...  8.22 us
    unnamed x32, local copies, waits for them, and re-layouts  6.66 us
    all_to_all x1, waiting for transfers between devices, spectral_part(): lax.all_to_all(inverse_x.astype(jnp.bfloat16), 'gx', split_axis=1, concat...  5.81 us
    all_to_all x1, starting transfers between devices, spectral_part(): lax.all_to_all(inverse_x.astype(jnp.bfloat16), 'gx', split_axis=1, concat...  5.71 us
  transfers between devices with their start and end apart: 8, of which 5 were waited for; matrix products, arithmetic and copies ran while one was open for 22% of the time, Pallas kernels for 0%

profile of v1, /device:TPU:1, one launch (start us, length us, event | category | flops | bytes accessed | tf_op | source)
XLA Modules:
  0.0 197.7 jit_solution(10743018874617079695)
XLA Ops:
  6.5 2.0 %fusion.100 = (bf16[1,16,64,128]{3,2,1,0:T(8,128)(2,1)}, bf16[1,16,64,128]{3,2,1,0:T(8,128)(2,1)}) fusion(bf16[4,16,64,128]{3,2,1,0:T(8,128)(2,1)} %param.4), kind=kLoop, calls=%fused_computation.177 | loop fusion | bytes 1048576 | tf_op jit(solution)/shard_map/slice | solution.py:18
  8.6 1.3 collective-permute-start.1
  9.8 5.4 %collective-permute-start = (bf16[1,16,64,128]{3,2,1,0:T(8,128)(2,1)}, bf16[1,16,64,128]{3,2,1,0:T(8,128)(2,1)}, u32[]{:S(2)}, u32[]{:S(2)}) collective-permute-start(bf16[1,16,64,128]{3,2,1,0:T(8,128)(2,1)} %get-tuple-element.10), channel_id=1, source_target_pairs={{0,8},{8,16},{16,24},{24,32},{32,40},{40,48},{48,56},{56,64},{64,7... | collective-permute-start | bytes 786440 | tf_op jit(solution)/shard_map/ppermute | solution.py:19
  15.3 0.8 broadcast_multiply_fusion.7
  16.0 1.5 convolution_bitcast_fusion.2
  17.6 1.2 fusion.20
  18.8 0.9 copy.18
  19.7 2.5 %convert_element_type.206 = bf16[2,4,8,64,1,64]{5,3,2,1,0,4:T(8,128)(2,1)} reshape(bf16[2,4,16,16,128]{4,3,2,1,0:T(8,128)(2,1)} %copy.18) | data formatting | bytes 1048576 | tf_op jit(solution)/shard_map/convert_element_type | solution.py:69
  23.0 0.7 maximum_bitcast_fusion.2
  23.6 1.4 maximum_bitcast_fusion.9
  25.0 1.3 dynamic-slice
  26.3 1.0 constant_dynamic-update-slice_fusion.2
  27.4 1.0 constant_dynamic-update-slice_fusion
  28.4 7.1 %collective-permute-start.2 = (bf16[6,1,64,128]{3,2,1,0:T(8,128)(2,1)S(1)}, bf16[6,1,64,128]{3,2,1,0:T(8,128)(2,1)S(1)}, u32[]{:S(2)}, u32[]{:S(2)}) collective-permute-start(bf16[6,1,64,128]{3,2,1,0:T(8,128)(2,1)S(1)} %get-tuple-element.7), channel_id=1, source_target_pairs={{0,1},{1,2},{2,3},{3,4},{4,5},{5,6},{6,7},{8,9},{9,10},{10,11},{11... | collective-permute-start | bytes 294920 | tf_op jit(solution)/shard_map/ppermute | solution.py:19
  35.5 2.9 %collective-permute-start.3 = (bf16[6,1,64,128]{3,2,1,0:T(8,128)(2,1)S(1)}, bf16[6,1,64,128]{3,2,1,0:T(8,128)(2,1)S(1)}, u32[]{:S(2)}, u32[]{:S(2)}) collective-permute-start(bf16[6,1,64,128]{3,2,1,0:T(8,128)(2,1)S(1)} %get-tuple-element.8), channel_id=1, source_target_pairs={{1,0},{2,1},{3,2},{4,3},{5,4},{6,5},{7,6},{9,8},{10,9},{11,10},{12... | collective-permute-start | bytes 294920 | tf_op jit(solution)/shard_map/ppermute | solution.py:20
  38.4 0.7 multiply_convert_fusion.2
  39.1 3.3 %collective-permute-done.3 = bf16[6,1,64,128]{3,2,1,0:T(8,128)(2,1)S(1)} collective-permute-done((bf16[6,1,64,128]{3,2,1,0:T(8,128)(2,1)S(1)}, bf16[6,1,64,128]{3,2,1,0:T(8,128)(2,1)S(1)}, u32[]{:S(2)}, u32[]{:S(2)}) %collective-permute-start.3) | collective-permute-done | bytes 98336 | tf_op jit(solution)/shard_map/ppermute | solution.py:20
  42.4 1.2 fusion.16
  43.6 0.9 fusion.98
  44.6 0.9 pad_maximum_fusion
  45.7 2.6 %fusion.41 = f32[4,16,64,128]{3,2,1,0:T(8,128)} fusion(bf16[6,18,64,384]{3,2,1,0:T(8,128)(2,1)S(1)} %pad_maximum_fusion, bf16[3,3,384,128]{3,2,1,0:T(8,128)(2,1)S(1)} %bitcast.232), kind=kOutput, calls=%fused_computation.56 | convolution fusion | flops 402653184 | bytes 7503872 | tf_op jit(solution)/shard_map/dot_general | solution.py:122
  48.4 2.3 %fusion.42 = f32[4,16,64,128]{3,2,1,0:T(8,128)} fusion(bf16[6,18,64,384]{3,2,1,0:T(8,128)(2,1)S(1)} %pad_maximum_fusion, bf16[3,3,384,128]{3,2,1,0:T(8,128)(2,1)S(1)} %bitcast.233), kind=kOutput, calls=%fused_computation.58 | convolution fusion | flops 402653184 | bytes 7503872 | tf_op jit(solution)/shard_map/dot_general | solution.py:122
  50.7 2.4 %fusion.43 = f32[4,16,64,128]{3,2,1,0:T(8,128)} fusion(bf16[6,18,64,384]{3,2,1,0:T(8,128)(2,1)S(1)} %pad_maximum_fusion, bf16[3,3,384,128]{3,2,1,0:T(8,128)(2,1)S(1)} %bitcast.234), kind=kOutput, calls=%fused_computation.60 | convolution fusion | flops 402653184 | bytes 7503872 | tf_op jit(solution)/shard_map/dot_general | solution.py:122
  53.0 57.0 %all-reduce.4.cloned.1.call-done = bf16[2,4,8,64,1,64]{5,3,2,1,0,4:T(8,128)(2,1)} async-done(((bf16[2,4,8,64,1,64]{5,3,2,1,0,4:T(8,128)(2,1)}), bf16[2,4,8,64,1,64]{5,3,2,1,0,4:T(8,128)(2,1)}) %all-reduce.4.cloned.1.call-update) | async-done | bytes 524304
  110.0 1.6 dynamic-slice_bitcast_fusion
  111.6 0.8 copy.77
  112.3 1.7 reshape.961
  114.0 10.7 %all-to-all-start = ((bf16[64,2,256]{2,1,0:T(2,128)(2,1)}), bf16[64,2,256]{2,1,0:T(2,128)(2,1)}, u32[]{:S(2)}, u32[]{:S(2)}) async-start(bf16[64,2,256]{2,1,0:T(2,128)(2,1)} %reshape.961), calls=%async_computation | async-start | bytes 131072 | tf_op jit(solution)/shard_map/all_to_all | solution.py:72
  124.7 4.3 %fusion.44 = f32[4,16,64,128]{3,2,1,0:T(8,128)} fusion(bf16[6,18,64,384]{3,2,1,0:T(8,128)(2,1)} %copy-done.1, bf16[3,3,384,128]{3,2,1,0:T(8,128)(2,1)S(1)} %bitcast.235), kind=kOutput, calls=%fused_computation.62 | convolution fusion | flops 402653184 | bytes 7503872 | tf_op jit(solution)/shard_map/dot_general | solution.py:122
  129.0 4.7 %all-to-all-done = bf16[64,2,256]{2,1,0:T(2,128)(2,1)} async-done(((bf16[64,2,256]{2,1,0:T(2,128)(2,1)}), bf16[64,2,256]{2,1,0:T(2,128)(2,1)}, u32[]{:S(2)}, u32[]{:S(2)}) %all-to-all-start) | async-done | bytes 65568 | tf_op jit(solution)/shard_map/all_to_all | solution.py:72
  133.7 1.7 reshape.962
  135.4 0.9 bitcast_bitcast_fusion
  137.2 0.6 fusion.22
  137.8 0.8 copy.25
  138.6 5.7 %all-to-all-start.1 = ((bf16[2,256,1,1,128]{4,0,3,2,1:T(2,128)(2,1)}), bf16[2,256,1,1,128]{4,0,3,2,1:T(2,128)(2,1)S(1)}, u32[]{:S(2)}, u32[]{:S(2)}) async-start(bf16[2,256,1,1,128]{4,0,3,2,1:T(2,128)(2,1)} %copy.25), calls=%async_computation.1 | async-start | bytes 262144 | tf_op jit(solution)/shard_map/all_to_all | solution.py:87
  144.3 4.2 %fusion.45 = f32[4,16,64,128]{3,2,1,0:T(8,128)} fusion(bf16[6,18,64,384]{3,2,1,0:T(8,128)(2,1)} %copy-done.1, bf16[3,3,384,128]{3,2,1,0:T(8,128)(2,1)S(1)} %bitcast.236), kind=kOutput, calls=%fused_computation.64 | convolution fusion | flops 402653184 | bytes 7503872 | tf_op jit(solution)/shard_map/dot_general | solution.py:122
  148.5 5.8 %all-to-all-done.1 = bf16[2,256,1,1,128]{4,0,3,2,1:T(2,128)(2,1)S(1)} async-done(((bf16[2,256,1,1,128]{4,0,3,2,1:T(2,128)(2,1)}), bf16[2,256,1,1,128]{4,0,3,2,1:T(2,128)(2,1)S(1)}, u32[]{:S(2)}, u32[]{:S(2)}) %all-to-all-start.1) | async-done | bytes 131104 | tf_op jit(solution)/shard_map/all_to_all | solution.py:87
  154.5 0.9 stack.127
  155.4 8.2 %all-to-all-start.2 = ((bf16[8,2,4,2,16,128]{5,4,3,2,1,0:T(8,128)(2,1)}), bf16[8,2,4,2,16,128]{5,4,3,2,1,0:T(8,128)(2,1)}, u32[]{:S(2)}, u32[]{:S(2)}) async-start(bf16[8,2,4,2,16,128]{5,4,3,2,1,0:T(8,128)(2,1)} %stack.127), calls=%async_computation.2 | async-start | bytes 1048576 | tf_op jit(solution)/shard_map/all_to_all | solution.py:94
  163.7 4.3 %fusion.46 = f32[4,16,64,128]{3,2,1,0:T(8,128)} fusion(bf16[6,18,64,384]{3,2,1,0:T(8,128)(2,1)} %copy-done.1, bf16[3,3,384,128]{3,2,1,0:T(8,128)(2,1)} %bitcast.228), kind=kOutput, calls=%fused_computation.66 | convolution fusion | flops 402653184 | bytes 7503872 | tf_op jit(solution)/shard_map/dot_general | solution.py:122
  168.0 4.2 %fusion.47 = f32[4,16,64,128]{3,2,1,0:T(8,128)} fusion(bf16[6,18,64,384]{3,2,1,0:T(8,128)(2,1)} %copy-done.1, bf16[3,3,384,128]{3,2,1,0:T(8,128)(2,1)} %bitcast.229), kind=kOutput, calls=%fused_computation.68 | convolution fusion | flops 402653184 | bytes 7503872 | tf_op jit(solution)/shard_map/dot_general | solution.py:122
  172.2 3.2 %fusion.48 = f32[4,16,64,128]{3,2,1,0:T(8,128)} fusion(bf16[6,18,64,384]{3,2,1,0:T(8,128)(2,1)S(1)} %bitcast.226, bf16[3,3,384,128]{3,2,1,0:T(8,128)(2,1)} %bitcast.230), kind=kOutput, calls=%fused_computation.70 | convolution fusion | flops 402653184 | bytes 7503872 | tf_op jit(solution)/shard_map/dot_general | solution.py:122
  175.4 3.7 %all-to-all-done.2 = bf16[8,2,4,2,16,128]{5,4,3,2,1,0:T(8,128)(2,1)} async-done(((bf16[8,2,4,2,16,128]{5,4,3,2,1,0:T(8,128)(2,1)}), bf16[8,2,4,2,16,128]{5,4,3,2,1,0:T(8,128)(2,1)}, u32[]{:S(2)}, u32[]{:S(2)}) %all-to-all-start.2) | async-done | bytes 524320 | tf_op jit(solution)/shard_map/all_to_all | solution.py:94
  179.1 1.2 copy.28
  180.4 0.6 fusion.19
  181.1 0.5 fusion.32
  181.5 0.6 copy-done.2
  182.1 8.8 %fusion.11 = bf16[4,16,64,128]{3,2,1,0:T(8,128)(2,1)} fusion(f32[64,4,16,128,1]{3,0,4,2,1:T(8,128)S(1)} %fusion.32, f32[4,16,64,128]{3,2,1,0:T(8,128)S(1)} %copy-done.2, f32[4,16,64,128]{3,2,1,0:T(8,128)S(1)} %copy-done.3, f32[4,16,64,128]{3,2,1,0:T(8,128)} %fusion.43, f32[4,16,64,128]{3,2,1,0:T(8,128)} %fusion.44, f32[4,16,64,128]{3,2,1,0:T(8,128)} %fusion.45, ...), kind=kOutput, calls=%fused_computation.15 | convolution fusion | flops 412614656 | bytes 25330176 | tf_op jit(solution)/shard_map/dot_general | solution.py:122
  (48 shorter events, 2.3 us)
Async XLA Ops:
  6.5 130.1 %copy-start = (bf16[1,64,2,64,128]{4,3,2,1,0:T(8,128)(2,1)S(1)}, bf16[1,64,2,64,128]{4,3,2,1,0:T(8,128)(2,1)}, u32[]{:S(2)}) copy-start(bf16[1,64,2,64,128]{4,3,2,1,0:T(8,128)(2,1)} %param.5) | copy-start | bytes 6291460
  6.5 103.5 %all-reduce.4.cloned.1.call-start = ((), (), s32[]{:S(2)}) async-start(), calls=%async_computation.3 | async-start | bytes 2097152
  8.6 18.9 %collective-permute-start.1 = (bf16[1,16,64,128]{3,2,1,0:T(8,128)(2,1)}, bf16[1,16,64,128]{3,2,1,0:T(8,128)(2,1)}, u32[]{:S(2)}, u32[]{:S(2)}) collective-permute-start(bf16[1,16,64,128]{3,2,1,0:T(8,128)(2,1)} %get-tuple-element.9), channel_id=1, source_target_pairs={{8,0},{16,8},{24,16},{32,24},{40,32},{48,40},{56,48},{64,56},{72,6... | collective-permute-start | bytes 786440 | tf_op jit(solution)/shard_map/ppermute | solution.py:20
  9.8 16.5 %collective-permute-start = (bf16[1,16,64,128]{3,2,1,0:T(8,128)(2,1)}, bf16[1,16,64,128]{3,2,1,0:T(8,128)(2,1)}, u32[]{:S(2)}, u32[]{:S(2)}) collective-permute-start(bf16[1,16,64,128]{3,2,1,0:T(8,128)(2,1)} %get-tuple-element.10), channel_id=1, source_target_pairs={{0,8},{8,16},{16,24},{24,32},{32,40},{40,48},{48,56},{56,64},{64,7... | collective-permute-start | bytes 786440 | tf_op jit(solution)/shard_map/ppermute | solution.py:19
  19.7 7.5 %copy-start.4 = (bf16[4,16,64,128]{3,2,1,0:T(8,128)(2,1)S(1)}, bf16[4,16,64,128]{3,2,1,0:T(8,128)(2,1)}, u32[]{:S(2)}) copy-start(bf16[4,16,64,128]{3,2,1,0:T(8,128)(2,1)} %param.4) | copy-start | bytes 3145732
  28.4 10.6 %collective-permute-start.2 = (bf16[6,1,64,128]{3,2,1,0:T(8,128)(2,1)S(1)}, bf16[6,1,64,128]{3,2,1,0:T(8,128)(2,1)S(1)}, u32[]{:S(2)}, u32[]{:S(2)}) collective-permute-start(bf16[6,1,64,128]{3,2,1,0:T(8,128)(2,1)S(1)} %get-tuple-element.7), channel_id=1, source_target_pairs={{0,1},{1,2},{2,3},{3,4},{4,5},{5,6},{6,7},{8,9},{9,10},{10,11},{11... | collective-permute-start | bytes 294920 | tf_op jit(solution)/shard_map/ppermute | solution.py:19
  35.5 6.8 %collective-permute-start.3 = (bf16[6,1,64,128]{3,2,1,0:T(8,128)(2,1)S(1)}, bf16[6,1,64,128]{3,2,1,0:T(8,128)(2,1)S(1)}, u32[]{:S(2)}, u32[]{:S(2)}) collective-permute-start(bf16[6,1,64,128]{3,2,1,0:T(8,128)(2,1)S(1)} %get-tuple-element.8), channel_id=1, source_target_pairs={{1,0},{2,1},{3,2},{4,3},{5,4},{6,5},{7,6},{9,8},{10,9},{11,10},{12... | collective-permute-start | bytes 294920 | tf_op jit(solution)/shard_map/ppermute | solution.py:20
  44.6 1.2 copy-start.5
  45.4 5.2 %copy-start.1 = (bf16[6,18,64,384]{3,2,1,0:T(8,128)(2,1)}, bf16[6,18,64,384]{3,2,1,0:T(8,128)(2,1)S(1)}, u32[]{:S(2)}) copy-start(bf16[6,18,64,384]{3,2,1,0:T(8,128)(2,1)S(1)} %pad_maximum_fusion) | copy-start | bytes 15925252
  114.0 19.7 %all-to-all-start = ((bf16[64,2,256]{2,1,0:T(2,128)(2,1)}), bf16[64,2,256]{2,1,0:T(2,128)(2,1)}, u32[]{:S(2)}, u32[]{:S(2)}) async-start(bf16[64,2,256]{2,1,0:T(2,128)(2,1)} %reshape.961), calls=%async_computation | async-start | bytes 131072 | tf_op jit(solution)/shard_map/all_to_all | solution.py:72
  124.7 11.7 %copy-start.6 = (f32[1,2,256,64]{2,3,1,0:T(8,128)S(1)}, f32[1,2,256,64]{2,3,1,0:T(8,128)}, u32[]{:S(2)}) copy-start(f32[1,2,256,64]{2,3,1,0:T(8,128)} %get-tuple-element.15) | copy-start | bytes 393220
  138.6 15.7 %all-to-all-start.1 = ((bf16[2,256,1,1,128]{4,0,3,2,1:T(2,128)(2,1)}), bf16[2,256,1,1,128]{4,0,3,2,1:T(2,128)(2,1)S(1)}, u32[]{:S(2)}, u32[]{:S(2)}) async-start(bf16[2,256,1,1,128]{4,0,3,2,1:T(2,128)(2,1)} %copy.25), calls=%async_computation.1 | async-start | bytes 262144 | tf_op jit(solution)/shard_map/all_to_all | solution.py:87
  155.4 16.8 %slice-start = ((s8[5308416]{0:T(1024)(128)(4,1)}), s8[1114112]{0:T(1024)(128)(4,1)S(1)}, s32[]{:S(2)}) async-start(s8[5308416]{0:T(1024)(128)(4,1)} %bitcast.225), calls=%async_computation.4 | async-start | bytes 2228224
  155.4 23.7 %all-to-all-start.2 = ((bf16[8,2,4,2,16,128]{5,4,3,2,1,0:T(8,128)(2,1)}), bf16[8,2,4,2,16,128]{5,4,3,2,1,0:T(8,128)(2,1)}, u32[]{:S(2)}, u32[]{:S(2)}) async-start(bf16[8,2,4,2,16,128]{5,4,3,2,1,0:T(8,128)(2,1)} %stack.127), calls=%async_computation.2 | async-start | bytes 1048576 | tf_op jit(solution)/shard_map/all_to_all | solution.py:94
  163.7 8.6 %slice-start.1 = ((s8[5308416]{0:T(1024)(128)(4,1)}), s8[4194304]{0:T(1024)(128)(4,1)S(1)}, s32[]{:S(2)}) async-start(s8[5308416]{0:T(1024)(128)(4,1)} %bitcast.225), calls=%async_computation.5 | async-start | bytes 8388608
  172.2 8.2 %copy-start.7 = (f32[1,2,16,16]{2,3,1,0:T(8,128)S(1)}, f32[1,2,16,16]{2,3,1,0:T(8,128)}, u32[]{:S(2)}) copy-start(f32[1,2,16,16]{2,3,1,0:T(8,128)} %get-tuple-element.19) | copy-start | bytes 6148
  175.4 5.6 %copy-start.8 = (bf16[1,16,64]{2,1,0:T(8,128)(2,1)S(1)}, bf16[1,16,64]{2,1,0:T(8,128)(2,1)}, u32[]{:S(2)}) copy-start(bf16[1,16,64]{2,1,0:T(8,128)(2,1)} %get-tuple-element.38) | copy-start | bytes 6148
  175.4 5.6 %copy-start.9 = (bf16[1,16,64]{2,1,0:T(8,128)(2,1)S(1)}, bf16[1,16,64]{2,1,0:T(8,128)(2,1)}, u32[]{:S(2)}) copy-start(bf16[1,16,64]{2,1,0:T(8,128)(2,1)} %get-tuple-element.39) | copy-start | bytes 6148
  179.1 2.4 %copy-start.3 = (f32[4,16,64,128]{3,2,1,0:T(8,128)S(1)}, f32[4,16,64,128]{3,2,1,0:T(8,128)}, u32[]{:S(2)}) copy-start(f32[4,16,64,128]{3,2,1,0:T(8,128)} %fusion.42) | copy-start | bytes 6291460
  180.4 1.7 copy-start.2
  180.4 1.7 copy-start.10
Sparse Core Ops, SparseCore 0:
  22.3 87.6 all-reduce.3
